TPU v7x, 512 devices: a whole 4x8x8 slice. The times are simulated.
512 devices in a mesh: row: 64 (over y_lo, z, x), col: 8 (over y_hi, core).
Axes of the slice: x: 4, y: 8 (y_hi: 4, y_lo: 2; y = y_hi * 2 + y_lo), z: 8, core: 2. Of those that a mesh axis runs over, the one named last changes fastest.
Arguments:
- orbitals: bfloat16 [16384, 2, 256], P(('row', 'col')), may hold values from -6 to 6
- kernel: bfloat16 [16384, 16384], P('row', 'col'), may hold values from -0.0029296875 to 0.0029296875
- basis: bfloat16 [16384, 2048], P('row'), may hold values from -0.046875 to 0.046875
Outputs:
- exchange: float32 [2048, 2, 256], P('row')
All inputs are finite; a program needn't handle non-finite values.
Results may differ from a plain program's by a relative error of at most 0.0041.
Values may be sent and summed in bfloat16 or wider, within the bound.
A program may use at most 64 MiB of HBM per device.

v0:
```python
import jax
import jax.numpy as jnp
from jax import lax
from jax.sharding import PartitionSpec as P


def body(orbitals, kernel, basis):
    row_orbitals = lax.all_gather(orbitals, "col", axis=0, tiled=True)
    point_rows = row_orbitals.shape[0]
    occupied = orbitals.shape[2]
    column_orbitals = lax.all_gather(orbitals, "row", axis=0, tiled=True)
    density = jnp.einsum(
        "psi,qsi->spq", row_orbitals, column_orbitals, preferred_element_type=jnp.float32
    )
    weighted = (density * kernel[None].astype(jnp.float32)).astype(jnp.bfloat16)
    applied = jnp.einsum(
        "spq,qsi->psi", weighted, column_orbitals, preferred_element_type=jnp.float32
    )
    out_rows = basis.shape[1] // lax.axis_size("row")
    summed = lax.psum(applied, "col").astype(jnp.bfloat16)
    flattened = summed.reshape(point_rows, -1)
    result = lax.psum_scatter(
        lax.dot_general(
            basis, flattened, (((0,), (0,)), ((), ())), preferred_element_type=jnp.float32
        ),
        "row",
        scatter_dimension=0,
        tiled=True,
    )
    return result.reshape(out_rows, 2, occupied)


def solution(mesh):
    return jax.shard_map(
        body,
        mesh=mesh,
        in_specs=(P(("row", "col"), None, None), P("row", "col"), P("row", None)),
        out_specs=P("row", None, None),
        check_vma=False,
    )
```

profile of v0, /device:TPU:56, one launch (start us, length us, event | category | flops | bytes accessed | tf_op | source)
XLA Modules:
  0.0 696.1 jit_solution(10531159770175762090)
XLA Ops:
  6.5 0.0 copy-start
  6.5 0.0 copy-start.1
  6.5 0.0 all-gather.2.cloned.1.call-start
  6.5 1.5 copy.9
  8.0 0.0 all-gather.2.cloned.1.call-update
  8.0 0.0 reduce-scatter.4.cloned.1.call-start
  8.1 1.5 convert_element_type.10
  9.6 0.0 copy-done.1
  9.6 14.7 %all_gather.6 = bf16[256,2,256]{2,1,0:T(2,128)(2,1)S(1)} all-gather(bf16[32,2,256]{2,1,0:T(2,128)(2,1)S(1)} %copy-done.1), channel_id=1, replica_groups=mesh['row'=64,'col'=8] {'col'}, dimensions={0}, use_global_device_ids=true | all-gather | bytes 294912 | tf_op jit(solution)/shard_map/all_gather | solution.py:8
  24.3 292.3 %all-gather.2.cloned.1.call-done = bf16[2048,2,256]{2,0,1:T(8,128)(2,1)} async-done(((bf16[32,2,256]{2,0,1:T(8,128)(2,1)}), bf16[2048,2,256]{2,0,1:T(8,128)(2,1)}) %all-gather.2.cloned.1.call-update) | async-done | bytes 2097168 | tf_op jit(solution)/shard_map/all_gather | solution.py:11
  316.6 4.3 fusion.1
  320.9 32.4 %all-reduce.1 = bf16[256,2,256]{2,0,1:T(8,128)(2,1)S(1)} all-reduce(f32[256,2,256]{2,0,1:T(8,128)} %fusion.1), channel_id=1, replica_groups=mesh['row'=64,'col'=8] {'col'}, use_global_device_ids=true, to_apply=%region_0.0 | all-reduce | flops 131072 | bytes 786432 | tf_op jit(solution)/shard_map/psum | solution.py:20
  353.3 0.1 copy.11
  353.5 0.0 copy-done
  353.5 2.7 convolution_bitcast_fusion
  356.2 5.3 copy.13
  361.5 0.0 reduce-scatter.4.cloned.1.call-update
  361.5 326.0 %reduce-scatter.4.cloned.1.call-done = f32[32,512]{1,0:T(8,128)} async-done(((f32[2048,512]{1,0:T(8,128)}), f32[32,512]{1,0:T(8,128)}) %reduce-scatter.4.cloned.1.call-update) | async-done | bytes 65552
  687.5 1.0 copy.14
  688.5 0.7 copy.12
Async XLA Ops:
  6.5 346.9 %copy-start = (bf16[256,2048]{1,0:T(8,128)(2,1)S(1)}, bf16[256,2048]{1,0:T(8,128)(2,1)}, u32[]{:S(2)}) copy-start(bf16[256,2048]{1,0:T(8,128)(2,1)} %param.5) | copy-start | bytes 3145732
  6.5 3.0 copy-start.1
  6.5 310.0 %all-gather.2.cloned.1.call-start = ((), (), s32[]{:S(2)}) async-start(), calls=%async_computation.1 | async-start | bytes 2129920 | tf_op jit(solution)/shard_map/all_gather | solution.py:11
  8.0 679.5 %reduce-scatter.4.cloned.1.call-start = ((), (), s32[]{:S(2)}) async-start(), calls=%async_computation.2 | async-start | bytes 4259840
Sparse Core Ops, SparseCore 0:
  9.4 307.0 all-gather.1
  361.6 325.8 reduce-scatter.3
where the time goes:
time: 697 us; the launch traced here: 696 us
  waiting for transfers between devices  618 us (89%)
  blocking collectives  47.2 us (7%)
  between operations  13.4 us (2%)
  local copies, waits for them, and re-layouts  8.66 us (1%)
  matrix products  6.99 us (1%)
    unnamed x3, waiting for transfers between devices  326 us
    all_gather x1, waiting for transfers between devices, body(): column_orbitals = lax.all_gather(orbitals, 'row', axis=0, tiled=True)  292 us
    psum x1, blocking collectives, body(): summed = lax.psum(applied, 'col').astype(jnp.bfloat16)  32.4 us
    all_gather x1, blocking collectives, body(): row_orbitals = lax.all_gather(orbitals, 'col', axis=0, tiled=True)  14.7 us
  transfers between devices with their start and end apart: 2, of which 2 were waited for; matrix products, arithmetic and copies ran while one was open for 0% of the time, Pallas kernels for 0%

commit v1 on v0

v1 whole, which is shorter than its diff:
```python
import jax
import jax.numpy as jnp
from jax import lax
from jax.experimental import pallas as pl
from jax.experimental.pallas import tpu as pltpu
from jax.sharding import PartitionSpec as P

MESH = pl.DeviceIdType.MESH
Y, Z, X = 2, 8, 4
H, K = 4, 2
ROWS, COLS = Y * Z * X, H * K
PIECE, WIDTH = 32, 512
POINTS = COLS * PIECE
BAND = X * PIECE
HOPS = (0, 1, 7, 2, 6, 3, 5, 4)
BF, F32 = jnp.bfloat16, jnp.float32


def kernel(
    orb_ref, kernel_ref, basis_ref, out_ref,
    col, rows, kern, basis, basis2, acc, packed, packed16, part, proj, proj16, xpart, zsum, zpart, ysum, ypart, fin,
    load_sem, zs, zr, xs, xr, ys, yr, ys2, yr2, xs2, xr2, hs, hr, ks, kr, cs, cr, rxs, rxr, rzs, rzr, rys, ryr, fs, fr,
):
    row, me = lax.axis_index("row"), lax.axis_index("col")
    yl, z, x = row // (Z * X), (row // X) % Z, row % X
    h, k = me // K, me % K

    def at_row(a, b, c):
        return (a * Z + b) * X + c

    def z_dev(d):
        return {"row": at_row(yl, (z + d) % Z, x)}

    def x_dev(e):
        return {"row": at_row(yl, z, (x + e) % X)}

    y_dev = {"row": at_row(1 - yl, z, x)}

    def c_at(dh, dk):
        return ((h + dh) % H) * K + (k + dk) % K

    def c_dev(dh, dk):
        return {"col": c_at(dh, dk)}

    PEERS = [(dh, dk) for dh in (2, 1, 3, 0) for dk in (0, 1) if (dh, dk) != (0, 0)]

    barrier = pltpu.get_barrier_semaphore()
    peers = [z_dev(d) for d in range(1, Z)] + [x_dev(e) for e in range(1, X)] + [y_dev] + [c_dev(*p) for p in PEERS]
    for p in peers:
        pl.semaphore_signal(barrier, inc=1, device_id=p, device_id_type=MESH)

    load_k = pltpu.make_async_copy(kernel_ref, kern, load_sem.at[0])
    load_b = pltpu.make_async_copy(basis_ref, basis, load_sem.at[1])
    load_k.start()
    load_b.start()
    mine = orb_ref[...]
    col[row] = mine
    rows[me] = mine
    pl.semaphore_wait(barrier, len(peers))

    sends = []

    def send(src, dst, s, r, dev):
        c = pltpu.make_async_remote_copy(src, dst, s, r, device_id=dev, device_id_type=MESH)
        c.start()
        sends.append(c)

    def arrived(dst, s, r, dev):
        pltpu.make_async_remote_copy(dst, dst, s, r, device_id=dev, device_id_type=MESH).wait_recv()

    TOP, BOT = pl.ds(0, PIECE // 2), pl.ds(PIECE // 2, PIECE // 2)

    for d in HOPS[1:]:
        send(col.at[row], col.at[row], zs.at[d], zr.at[d], z_dev(d))
    for dh in (2, 1, 3):
        send(rows.at[me], rows.at[me], hs.at[dh], hr.at[dh], c_dev(dh, 0))
    send(rows.at[me], rows.at[me], ks.at[0], kr.at[0], c_dev(0, 1))

    def spread(d):
        i = at_row(yl, (z - d + Z) % Z, x)
        b = col.at[i]
        for e in (2, 1, 3):
            send(b, b, xs.at[d, e], xr.at[d, e], x_dev(e))
        send(b, b, ys.at[d], yr.at[d], y_dev)

    def stage1(d):
        if d:
            i = at_row(yl, (z - d + Z) % Z, x)
            arrived(col.at[i], zs.at[d], zr.at[d], z_dev(d))
        spread(d)

    def stage2(d):
        zb = (z - d + Z) % Z
        for e in (1, 3, 2):
            b = col.at[at_row(yl, zb, (x - e + X) % X)]
            arrived(b, xs.at[d, e], xr.at[d, e], x_dev(e))
            send(b.at[TOP], b.at[TOP], ys2.at[d, e], yr2.at[d, e], y_dev)
        b = col.at[at_row(1 - yl, zb, x)]
        arrived(b, ys.at[d], yr.at[d], y_dev)
        for e in (2, 1, 3):
            send(b.at[BOT], b.at[BOT], xs2.at[d, e], xr2.at[d, e], x_dev(e))

    def stage3(d):
        zb = (z - d + Z) % Z
        for e in (1, 3, 2):
            b = col.at[at_row(1 - yl, zb, (x - e + X) % X)]
            arrived(b.at[TOP], ys2.at[d, e], yr2.at[d, e], y_dev)
            arrived(b.at[BOT], xs2.at[d, e], xr2.at[d, e], x_dev(e))

    def compute(y_at, d, first=False):
        band = y_at * Z + (z - d + Z) % Z
        c = col[pl.ds(band * X, X)].reshape(BAND, WIDTH)
        kk = kern[:, pl.ds(pl.multiple_of(band * BAND, BAND), BAND)].astype(F32)
        for s in range(2):
            sl = slice(s * 256, s * 256 + 256)
            r = rows[:, :, sl].reshape(POINTS, 256)
            den = lax.dot_general(r, c[:, sl], (((1,), (1,)), ((), ())), preferred_element_type=F32)
            w = (den * kk).astype(BF)
            t = jnp.dot(w, c[:, sl], preferred_element_type=F32)
            if first:
                acc[:, sl] = t
            else:
                acc[:, sl] += t

    stage1(HOPS[0])
    load_b.wait()
    for y_at in range(Y):
        basis2[:, y_at * POINTS:(y_at + 1) * POINTS] = basis[:, y_at * 1024:(y_at + 1) * 1024].T
    for dh in (1, 3, 2):
        b = rows.at[c_at(H - dh, 0)]
        arrived(b, hs.at[dh], hr.at[dh], c_dev(dh, 0))
        send(b, b, ks.at[dh], kr.at[dh], c_dev(0, 1))
    stage1(HOPS[1])
    stage1(HOPS[2])
    stage2(HOPS[0])
    for dh in range(H):
        arrived(rows.at[c_at(H - dh, 1)], ks.at[dh], kr.at[dh], c_dev(0, 1))
    load_k.wait()
    for n in range(3, Z + 3):
        if n < Z:
            stage1(HOPS[n])
        if 1 <= n - 2 < Z:
            stage2(HOPS[n - 2])
        if n - 3 < Z:
            compute(yl, HOPS[n - 3], n == 3)
            stage3(HOPS[n - 3])
            compute(1 - yl, HOPS[n - 3])

    low = lax.broadcasted_iota(jnp.int32, (128, 128), 1) < 64
    for q in range(H):
        top, bot = acc[0:128, q * 128:q * 128 + 128], acc[128:256, q * 128:q * 128 + 128]
        for j, v in enumerate((jnp.where(low, top, pltpu.roll(bot, 64, 1)), jnp.where(low, pltpu.roll(top, 64, 1), bot))):
            packed[2 * q + j] = v
            packed16[2 * q + j] = v.astype(BF)
    for dh, dk in PEERS:
        n = dh * K + dk
        send(packed16.at[c_at(dh, dk)], part.at[n], cs.at[n], cr.at[n], c_dev(dh, dk))
    total = packed[me]
    for dh, dk in reversed(PEERS):
        n = dh * K + dk
        arrived(part.at[n], cs.at[n], cr.at[n], c_dev(dh, dk))
        total += part[n].astype(F32)

    t, tr = total.astype(BF).astype(F32), pltpu.roll(total.astype(BF).astype(F32), 64, 1)
    zero = jnp.zeros_like(t)
    rhs = jnp.concatenate([jnp.where(low, t, zero), jnp.where(low, tr, zero), jnp.where(low, zero, tr), jnp.where(low, zero, t)], axis=0).astype(BF)
    e = jnp.dot(basis2[...], rhs, preferred_element_type=F32).reshape(Z, X, PIECE, 128)
    proj[...] = e
    proj16[...] = e.astype(BF)

    for n in (2, 1, 3):
        send(proj16.at[:, (x + n) % X], xpart.at[n], rxs.at[n], rxr.at[n], x_dev(n))
    sums = proj[:, x]
    for n in (1, 3, 2):
        arrived(xpart.at[n], rxs.at[n], rxr.at[n], x_dev(n))
        sums += xpart[n].astype(F32)
    zsum[...] = sums
    for d in (4, 3, 5, 2, 6, 1, 7):
        send(zsum.at[(z + d) % Z], zpart.at[d], rzs.at[d], rzr.at[d], z_dev(d))
    sums = zsum[z]
    for d in HOPS[1:]:
        arrived(zpart.at[d], rzs.at[d], rzr.at[d], z_dev(d))
        sums += zpart[d]
    ysum[...] = sums
    send(ysum, ypart, rys.at[0], ryr.at[0], y_dev)
    arrived(ypart, rys.at[0], ryr.at[0], y_dev)
    sums += ypart[...]

    v = jnp.where(yl == 0, sums, pltpu.roll(sums, 64, 1))
    low = low[0:16]
    fin[me] = jnp.where(low, v[0:16], pltpu.roll(v[16:32], 64, 1))
    for dh, dk in PEERS:
        n = dh * K + dk
        send(fin.at[me], fin.at[me], fs.at[n], fr.at[n], c_dev(dh, dk))
    for dh, dk in reversed(PEERS):
        n = dh * K + dk
        arrived(fin.at[c_at(H - dh, dk)], fs.at[n], fr.at[n], c_dev(dh, dk))
    for q in range(H):
        a, b = fin[2 * q], fin[2 * q + 1]
        out_ref[0:16, q * 128:q * 128 + 128] = jnp.where(low, a, pltpu.roll(b, 64, 1))
        out_ref[16:32, q * 128:q * 128 + 128] = jnp.where(low, pltpu.roll(a, 64, 1), b)
    for c in sends:
        c.wait_send()


def body(orbitals, kern, basis):
    V, D = pltpu.VMEM, pltpu.SemaphoreType.DMA
    out = pl.pallas_call(
        kernel,
        out_shape=jax.ShapeDtypeStruct((PIECE, WIDTH), F32),
        in_specs=[pl.BlockSpec(memory_space=pltpu.VMEM), pl.BlockSpec(memory_space=pl.ANY), pl.BlockSpec(memory_space=pl.ANY)],
        out_specs=pl.BlockSpec(memory_space=pltpu.VMEM),
        scratch_shapes=[
            V((ROWS, PIECE, WIDTH), BF), V((COLS, PIECE, WIDTH), BF), V((POINTS, 2048), BF), V((POINTS, 2048), BF),
            V((1024, 512), BF), V((POINTS, WIDTH), F32), V((COLS, 128, 128), F32), V((COLS, 128, 128), BF),
            V((COLS, 128, 128), BF), V((Z, X, PIECE, 128), F32), V((Z, X, PIECE, 128), BF), V((X, Z, PIECE, 128), BF),
            V((Z, PIECE, 128), F32), V((Z, PIECE, 128), F32), V((PIECE, 128), F32), V((PIECE, 128), F32), V((COLS, 16, 128), F32),
            D((2,)),
            D((Z,)), D((Z,)), D((Z, X)), D((Z, X)), D((Z,)), D((Z,)), D((Z, X)), D((Z, X)), D((Z, X)), D((Z, X)),
            D((H,)), D((H,)), D((H,)), D((H,)), D((COLS,)), D((COLS,)), D((X,)), D((X,)), D((Z,)), D((Z,)), D((1,)), D((1,)),
            D((COLS,)), D((COLS,)),
        ],
        compiler_params=pltpu.CompilerParams(collective_id=0, has_side_effects=True, vmem_limit_bytes=48 << 20),
        cost_estimate=pl.CostEstimate(flops=1_300_000_000, bytes_accessed=2_300_000, transcendentals=0),
        name="exchange",
    )(orbitals.reshape(PIECE, WIDTH), kern, basis)
    return out.reshape(PIECE, 2, WIDTH // 2)


def solution(mesh):
    return jax.shard_map(
        body,
        mesh=mesh,
        in_specs=(P(("row", "col"), None, None), P("row", "col"), P("row", None)),
        out_specs=P("row", None, None),
        check_vma=False,
    )
```

time: 697 us -> 76.6 us (0.11)
  the two profiles are of different devices: /device:TPU:56 before, /device:TPU:1 now
where the time goes in v1:
time: 76.6 us; the launch traced here: 76.3 us
  Pallas kernels  72.4 us (95%)
  local copies, waits for them, and re-layouts  3.88 us (5%)
    pallas_call x1, Pallas kernels, body(): pl.pallas_call(kernel, out_shape=jax.ShapeDtypeStruct((PIECE, WIDTH), F32...  72.4 us
    unnamed x5, local copies, waits for them, and re-layouts  3.21 us

profile of v1, /device:TPU:1, one launch (start us, length us, event | category | flops | bytes accessed | tf_op | source)
XLA Modules:
  0.0 76.3 jit_solution(8631173194452872661)
XLA Ops:
  0.0 0.8 %copy.4 = bf16[4,8,2,256]{3,1,2,0:T(8,128)(2,1)S(1)} copy(bf16[4,8,2,256]{3,2,1,0:T(2,128)(2,1)} %bitcast.3) | data formatting | bytes 65536
  0.8 0.0 copy-start
  0.8 1.2 %copy-done = bf16[256,2048]{1,0:T(8,128)(2,1)S(1)} copy-done((bf16[256,2048]{1,0:T(8,128)(2,1)S(1)}, bf16[256,2048]{1,0:T(8,128)(2,1)}, u32[]{:S(2)}) %copy-start) | copy-done | bytes 1048600
  2.0 0.0 copy-start.1
  2.0 1.2 %copy-done.1 = bf16[256,2048]{1,0:T(8,128)(2,1)S(1)} copy-done((bf16[256,2048]{1,0:T(8,128)(2,1)S(1)}, bf16[256,2048]{1,0:T(8,128)(2,1)}, u32[]{:S(2)}) %copy-start.1) | copy-done | bytes 1048600
  3.2 72.4 %exchange.1 = f32[32,512]{1,0:T(8,128)S(1)} custom-call(bf16[32,512]{1,0:T(8,128)(2,1)S(1)} %bitcast.2, bf16[256,2048]{1,0:T(8,128)(2,1)S(1)} %copy-done, bf16[256,2048]{1,0:T(8,128)(2,1)S(1)} %copy-done.1), custom_call_target="tpu_custom_call" | custom-call | flops 1300000000 | bytes 2300000 | tf_op jit(solution)/shard_map/exchange/pallas_call | solution.py:208
  75.6 0.7 reshape.7
Async XLA Ops:
  0.8 1.2 %copy-start = (bf16[256,2048]{1,0:T(8,128)(2,1)S(1)}, bf16[256,2048]{1,0:T(8,128)(2,1)}, u32[]{:S(2)}) copy-start(bf16[256,2048]{1,0:T(8,128)(2,1)} %kernel_ref.1) | copy-start | bytes 3145732
  2.0 1.2 %copy-start.1 = (bf16[256,2048]{1,0:T(8,128)(2,1)S(1)}, bf16[256,2048]{1,0:T(8,128)(2,1)}, u32[]{:S(2)}) copy-start(bf16[256,2048]{1,0:T(8,128)(2,1)} %basis_ref.1) | copy-start | bytes 3145732

commit v2 on v0

v2 whole, which is shorter than its diff:
```python
import jax
import jax.numpy as jnp
from jax import lax
from jax.experimental import pallas as pl
from jax.experimental.pallas import tpu as pltpu
from jax.sharding import PartitionSpec as P

MESH = pl.DeviceIdType.MESH
Y, Z, X = 2, 8, 4
H, K = 4, 2
ROWS, COLS = Y * Z * X, H * K
PIECE, WIDTH = 32, 512
POINTS = COLS * PIECE
BAND = X * PIECE
HOPS = (0, 1, 7, 2, 6, 3, 5, 4)
FAR = 4
SCHEDULE = (
    "s0", "t0", "B", "s1", "s7", "c0", "s2", "s6", "c1", "s3", "s5", "R",
    "c7", "s4", "Z", "r0", "c2", "c6", "r1", "r7", "I", "c3", "n0", "c5",
    "r2", "f0", "r6", "n1", "c4", "t1", "t7", "n7", "t4", "t2", "r3", "n2",
    "t6", "r5", "n6", "t3", "t5", "f1", "r4", "f7", "n3", "n5", "f2", "n4",
    "f6", "f3", "f5", "f4",
)
BF, F32 = jnp.bfloat16, jnp.float32


def kernel(
    orb_ref, kernel_ref, basis_ref, out_ref,
    orb, col, rows, kern, basis, basis2, acc, packed, pairs, send16, part, proj, proj16, xpart, zsum, zpart, fin,
    load_sem, sent, zr, zr2, xr, xr3, yr, lr, hr, kr, pr, cr, rxr, rzr, fr,
):
    row, me = lax.axis_index("row"), lax.axis_index("col")
    yl, z, x = row // (Z * X), (row // X) % Z, row % X
    h, k = me // K, me % K

    def at_row(a, b, c):
        return (a * Z + b) * X + c

    def z_dev(d):
        return {"row": at_row(yl, (z + d) % Z, x)}

    def x_dev(e):
        return {"row": at_row(yl, z, (x + e) % X)}

    y_dev = {"row": at_row(1 - yl, z, x)}

    def xy_dev(n):
        return {"row": at_row((yl + n // X) % Y, z, (x + n % X) % X)}

    def c_at(dh, dk):
        return ((h + dh) % H) * K + (k + dk) % K

    def c_dev(dh, dk):
        return {"col": c_at(dh, dk)}

    PEERS = [(dh, dk) for dh in (2, 1, 3, 0) for dk in (0, 1) if (dh, dk) != (0, 0)]

    barrier = pltpu.get_barrier_semaphore()
    peers = [z_dev(d) for d in range(1, Z)] + [xy_dev(n) for n in range(1, X * Y)] + [c_dev(*p) for p in PEERS]
    for p in peers:
        pl.semaphore_signal(barrier, inc=1, device_id=p, device_id_type=MESH)

    load_o = pltpu.make_async_copy(orb_ref, orb, load_sem.at[0])
    load_k = pltpu.make_async_copy(kernel_ref, kern, load_sem.at[1])
    load_b = pltpu.make_async_copy(basis_ref, basis, load_sem.at[2])
    load_o.start()
    load_k.start()
    load_b.start()
    load_o.wait()
    for s in range(2):
        mine = orb[:, s, :]
        col[row, :, s * 256:s * 256 + 256] = mine
        rows[me, :, s * 256:s * 256 + 256] = mine
    pl.semaphore_wait(barrier, len(peers))

    def send(src, dst, group, arrival, dev):
        pltpu.make_async_remote_copy(src, dst, sent.at[group], arrival, device_id=dev, device_id_type=MESH).start()

    def arrived(like, arrival):
        pltpu.make_async_copy(like, like, arrival).wait()

    HALVES = pl.ds(0, 256), pl.ds(256, 256)

    def block(y_at, d, e=0):
        return col.at[at_row(y_at, (z - d + Z) % Z, (x - e + X) % X)]

    own = col.at[row]
    send(own, own, 0, yr.at[0], y_dev)
    for d in HOPS[1:]:
        send(own, own, 0, zr.at[d], z_dev(d))
    for dh in (2, 1, 3):
        send(rows.at[me], rows.at[me], 1, hr.at[dh], c_dev(dh, 0))
    send(rows.at[me], rows.at[me], 1, kr.at[0], c_dev(0, 1))

    def spread(d):
        b = block(yl, d)
        if d:
            arrived(b, zr.at[d])
        for e in (1, 3):
            send(b, b, 2, xr.at[d], x_dev(e))
        if d == FAR:
            send(b, b, 0, yr.at[1], y_dev)

    def cross(d):
        arrived(col.at[pl.ds(0, 2)], xr.at[d])
        for n, e in enumerate((1, 3)):
            half = block(yl, d, e).at[:, HALVES[n]]
            send(half, half, 3, xr3.at[d], x_dev(e))
        for e in (1, 3):
            half = block(yl, d, e).at[:, HALVES[0]]
            send(half, half, 4, lr.at[d], y_dev)

    def relay(d):
        b = block(yl, d, 2)
        arrived(b, xr3.at[d])
        send(b, b, 5, lr.at[d], y_dev)

    def fan():
        b = block(1 - yl, 0)
        for d in HOPS[1:-1]:
            send(b, b, 1, zr2.at[d], z_dev(d))

    def spread2(d):
        b = block(1 - yl, d)
        arrived(b, yr.at[d // FAR] if d in (0, FAR) else zr2.at[d])
        half = b.at[:, HALVES[1]]
        for e in (1, 3):
            send(half, half, 6, lr.at[d], x_dev(e))

    def last(d):
        arrived(col.at[pl.ds(0, 3)], lr.at[d])

    def rows_on():
        for dh in (1, 3, 2):
            b = rows.at[c_at(H - dh, 0)]
            arrived(b, hr.at[dh])
            send(b, b, 1, kr.at[0], c_dev(0, 1))

    def rows_in():
        arrived(rows.at[pl.ds(0, 4)], kr.at[0])
        load_k.wait()

    def prepare():
        load_b.wait()
        for half in range(2):
            t = basis[:, half * 1024:half * 1024 + 1024].T.reshape(ROWS // 2, 2, PIECE // 2, POINTS)
            for q in range(2):
                basis2[half * 512:half * 512 + 512, q * POINTS:q * POINTS + POINTS] = t[:, q].reshape(512, POINTS)

    def compute(y_at, d, first=False):
        band = y_at * Z + (z - d + Z) % Z
        c = col[pl.ds(band * X, X)].reshape(BAND, WIDTH)
        kk = kern[:, pl.ds(pl.multiple_of(band * BAND, BAND), BAND)].astype(F32)
        for s in range(2):
            sl = slice(s * 256, s * 256 + 256)
            r = rows[:, :, sl].reshape(POINTS, 256)
            den = lax.dot_general(r, c[:, sl], (((1,), (1,)), ((), ())), preferred_element_type=F32)
            w = (den * kk).astype(BF)
            t = jnp.dot(w, c[:, sl], preferred_element_type=F32)
            if first:
                acc[:, sl] = t
            else:
                acc[:, sl] += t

    started = []

    def near(d):
        compute(yl, d, not started)
        started.append(d)

    def far(d):
        last(d)
        compute(1 - yl, d)

    steps = {"s": spread, "c": cross, "r": relay, "t": spread2, "n": near, "f": far, "Z": lambda _: fan(), "R": lambda _: rows_on(), "I": lambda _: rows_in(), "B": lambda _: prepare()}
    for step in SCHEDULE:
        steps[step[0]](int(step[1:] or 0))

    low = lax.broadcasted_iota(jnp.int32, (128, 128), 1) < 64
    for q in range(H):
        top, bot = acc[0:128, q * 128:q * 128 + 128], acc[128:256, q * 128:q * 128 + 128]
        packed[q, 0] = jnp.where(low, top, pltpu.roll(bot, 64, 1))
        packed[q, 1] = jnp.where(low, pltpu.roll(top, 64, 1), bot)
    for dh in (2, 1, 3, 0):
        send(packed.at[(h + dh) % H, 1 - k], pairs.at[dh], 7, pr.at[dh], c_dev(0, 1))
    for dh in (2, 1, 3):
        arrived(pairs.at[dh], pr.at[dh])
        send16[dh] = (packed[(h + dh) % H, k] + pairs[dh]).astype(BF)
        send(send16.at[dh], part.at[dh - 1], 8, cr.at[0], c_dev(dh, 0))
    arrived(pairs.at[0], pr.at[0])
    total = packed[h, k] + pairs[0]
    arrived(part, cr.at[0])
    for n in range(H - 1):
        total += part[n].astype(F32)

    t, tr = total.astype(BF).astype(F32), pltpu.roll(total.astype(BF).astype(F32), 64, 1)
    zero = jnp.zeros_like(t)
    rhs = jnp.concatenate([jnp.where(low, t, zero), jnp.where(low, tr, zero), jnp.where(low, zero, tr), jnp.where(low, zero, t)], axis=0).astype(BF)
    e = jnp.dot(basis2[...], rhs, preferred_element_type=F32).reshape(Y, Z, X, PIECE // 2, 128)
    proj[...] = e
    proj16[...] = e.astype(BF)

    for n in (6, 5, 7, 2, 4, 1, 3):
        send(proj16.at[(yl + n // X) % Y, :, (x + n % X) % X], xpart.at[n - 1], 9, rxr.at[0], xy_dev(n))
    sums = proj[yl, :, x]
    arrived(xpart, rxr.at[0])
    for n in range(X * Y - 1):
        sums += xpart[n].astype(F32)
    zsum[...] = sums
    for d in (4, 3, 5, 2, 6, 1, 7):
        send(zsum.at[(z + d) % Z], zpart.at[d - 1], 10, rzr.at[0], z_dev(d))
    sums = zsum[z]
    arrived(zpart, rzr.at[0])
    for n in range(Z - 1):
        sums += zpart[n]

    fin[me] = sums
    low = low[0:16]
    for dh, dk in PEERS:
        send(fin.at[me], fin.at[me], 11, fr.at[0], c_dev(dh, dk))
    arrived(fin.at[pl.ds(0, COLS - 1)], fr.at[0])
    for q in range(H):
        a, b = fin[2 * q], fin[2 * q + 1]
        sl = slice(q % 2 * 128, q % 2 * 128 + 128)
        out_ref[0:16, q // 2, sl] = jnp.where(low, a, pltpu.roll(b, 64, 1))
        out_ref[16:32, q // 2, sl] = jnp.where(low, pltpu.roll(a, 64, 1), b)
    arrived(col.at[pl.ds(0, 9)], sent.at[0])
    arrived(col.at[pl.ds(0, 13)], sent.at[1])
    arrived(col.at[pl.ds(0, 16)], sent.at[2])
    for n in (3, 4, 5, 6):
        arrived(col.at[pl.ds(0, 8)], sent.at[n])
    arrived(pairs, sent.at[7])
    arrived(part, sent.at[8])
    arrived(xpart, sent.at[9])
    arrived(zpart, sent.at[10])
    arrived(fin.at[pl.ds(0, COLS - 1)], sent.at[11])


def body(orbitals, kern, basis):
    V, D = pltpu.VMEM, pltpu.SemaphoreType.DMA
    return pl.pallas_call(
        kernel,
        out_shape=jax.ShapeDtypeStruct((PIECE, 2, WIDTH // 2), F32),
        in_specs=[pl.BlockSpec(memory_space=pltpu.HBM), pl.BlockSpec(memory_space=pltpu.HBM), pl.BlockSpec(memory_space=pltpu.HBM)],
        out_specs=pl.BlockSpec(memory_space=pltpu.VMEM),
        scratch_shapes=[
            V((PIECE, 2, WIDTH // 2), BF), V((ROWS, PIECE, WIDTH), BF), V((COLS, PIECE, WIDTH), BF), V((POINTS, 2048), BF), V((POINTS, 2048), BF),
            V((1024, 512), BF), V((POINTS, WIDTH), F32), V((H, K, 128, 128), F32), V((H, 128, 128), F32), V((H, 128, 128), BF),
            V((H - 1, 128, 128), BF), V((Y, Z, X, 16, 128), F32), V((Y, Z, X, 16, 128), BF), V((X * Y - 1, Z, 16, 128), BF),
            V((Z, 16, 128), F32), V((Z - 1, 16, 128), F32), V((COLS, 16, 128), F32),
            D((3,)), D((12,)), D((Z,)), D((Z,)), D((Z,)), D((Z,)), D((2,)), D((Z,)), D((H,)), D((1,)), D((H,)), D((1,)), D((1,)), D((1,)), D((1,)),
        ],
        compiler_params=pltpu.CompilerParams(collective_id=0, has_side_effects=True, vmem_limit_bytes=61 << 20),
        cost_estimate=pl.CostEstimate(flops=1_300_000_000, bytes_accessed=2_300_000, transcendentals=0),
        name="exchange",
    )(orbitals, kern, basis)


def solution(mesh):
    return jax.shard_map(
        body,
        mesh=mesh,
        in_specs=(P(("row", "col"), None, None), P("row", "col"), P("row", None)),
        out_specs=P("row", None, None),
        check_vma=False,
    )
```

time: 697 us -> 60.9 us (0.09)
  the two profiles are of different devices: /device:TPU:56 before, /device:TPU:1 now
where the time goes in v2:
time: 60.9 us; the launch traced here: 60.7 us
  Pallas kernels  59.2 us (97%)
  local copies, waits for them, and re-layouts  1.47 us (2%)
    pallas_call x1, Pallas kernels, body(): pl.pallas_call(kernel, out_shape=jax.ShapeDtypeStruct((PIECE, 2, WIDTH //...  59.2 us
    unnamed x1, local copies, waits for them, and re-layouts  1.47 us

profile of v2, /device:TPU:1, one launch (start us, length us, event | category | flops | bytes accessed | tf_op | source)
XLA Modules:
  0.0 60.7 jit_solution(14479041567480583205)
XLA Ops:
  0.0 59.2 %exchange.1 = f32[32,2,256]{2,1,0:T(2,128)} custom-call(bf16[32,2,256]{2,1,0:T(2,128)(2,1)} %orb_ref.1, bf16[256,2048]{1,0:T(8,128)(2,1)} %kernel_ref.1, bf16[256,2048]{1,0:T(8,128)(2,1)} %basis_ref.1), custom_call_target="tpu_custom_call" | custom-call | flops 1300000000 | bytes 2300000 | tf_op jit(solution)/shard_map/exchange/pallas_call | solution.py:241
  59.2 1.5 %copy.5 = f32[32,2,256]{2,1,0:T(2,128)} copy(f32[32,2,256]{2,1,0:T(2,128)} %exchange.1) | data formatting | bytes 131072

commit v3 on v2

--- a/solution.py
+++ b/solution.py
@@ -196,22 +196,34 @@
     t, tr = total.astype(BF).astype(F32), pltpu.roll(total.astype(BF).astype(F32), 64, 1)
     zero = jnp.zeros_like(t)
     rhs = jnp.concatenate([jnp.where(low, t, zero), jnp.where(low, tr, zero), jnp.where(low, zero, tr), jnp.where(low, zero, t)], axis=0).astype(BF)
-    e = jnp.dot(basis2[...], rhs, preferred_element_type=F32).reshape(Y, Z, X, PIECE // 2, 128)
-    proj[...] = e
-    proj16[...] = e.astype(BF)
-
-    for n in (6, 5, 7, 2, 4, 1, 3):
-        send(proj16.at[(yl + n // X) % Y, :, (x + n % X) % X], xpart.at[n - 1], 9, rxr.at[0], xy_dev(n))
-    sums = proj[yl, :, x]
-    arrived(xpart, rxr.at[0])
-    for n in range(X * Y - 1):
-        sums += xpart[n].astype(F32)
-    zsum[...] = sums
-    for d in (4, 3, 5, 2, 6, 1, 7):
-        send(zsum.at[(z + d) % Z], zpart.at[d - 1], 10, rzr.at[0], z_dev(d))
-    sums = zsum[z]
-    arrived(zpart, rzr.at[0])
-    for n in range(Z - 1):
+    HALF = Z // 2
+    for half in range(2):
+        zz = slice(half * HALF, half * HALF + HALF)
+        for y_at in range(Y):
+            r0 = (y_at * Z + half * HALF) * X * 16
+            e = jnp.dot(basis2[r0:r0 + HALF * X * 16], rhs, preferred_element_type=F32).reshape(HALF, X, 16, 128)
+            proj[y_at, zz] = e
+            proj16[y_at, zz] = e.astype(BF)
+        for n in (6, 5, 7, 2, 4, 1, 3):
+            piece = proj16.at[(yl + n // X) % Y, pl.ds(half * HALF, HALF), (x + n % X) % X]
+            send(piece, xpart.at[half, n - 1], 9, rxr.at[half], xy_dev(n))
+    for half in range(2):
+        zz = slice(half * HALF, half * HALF + HALF)
+        sums = proj[yl, zz, x]
+        arrived(xpart.at[half], rxr.at[half])
+        for n in range(X * Y - 1):
+            sums += xpart[half, n].astype(F32)
+        zsum[zz] = sums
+        for t in range(half * HALF, half * HALF + HALF):
+
+            @pl.when(z != t)
+            def _(t=t):
+                send(zsum.at[t], zpart.at[z], 10, rzr.at[0], {"row": at_row(yl, t, x)})
+
+    zpart[z] = zsum[z]
+    arrived(zpart.at[pl.ds(0, Z - 1)], rzr.at[0])
+    sums = zpart[0]
+    for n in range(1, Z):
         sums += zpart[n]
 
     fin[me] = sums
@@ -232,7 +244,7 @@
     arrived(pairs, sent.at[7])
     arrived(part, sent.at[8])
     arrived(xpart, sent.at[9])
-    arrived(zpart, sent.at[10])
+    arrived(zpart.at[pl.ds(0, Z - 1)], sent.at[10])
     arrived(fin.at[pl.ds(0, COLS - 1)], sent.at[11])
 
 
@@ -246,11 +258,11 @@
         scratch_shapes=[
             V((PIECE, 2, WIDTH // 2), BF), V((ROWS, PIECE, WIDTH), BF), V((COLS, PIECE, WIDTH), BF), V((POINTS, 2048), BF), V((POINTS, 2048), BF),
             V((1024, 512), BF), V((POINTS, WIDTH), F32), V((H, K, 128, 128), F32), V((H, 128, 128), F32), V((H, 128, 128), BF),
-            V((H - 1, 128, 128), BF), V((Y, Z, X, 16, 128), F32), V((Y, Z, X, 16, 128), BF), V((X * Y - 1, Z, 16, 128), BF),
-            V((Z, 16, 128), F32), V((Z - 1, 16, 128), F32), V((COLS, 16, 128), F32),
-            D((3,)), D((12,)), D((Z,)), D((Z,)), D((Z,)), D((Z,)), D((2,)), D((Z,)), D((H,)), D((1,)), D((H,)), D((1,)), D((1,)), D((1,)), D((1,)),
+            V((H - 1, 128, 128), BF), V((Y, Z, X, 16, 128), F32), V((Y, Z, X, 16, 128), BF), V((2, X * Y - 1, Z // 2, 16, 128), BF),
+            V((Z, 16, 128), F32), V((Z, 16, 128), F32), V((COLS, 16, 128), F32),
+            D((3,)), D((12,)), D((Z,)), D((Z,)), D((Z,)), D((Z,)), D((2,)), D((Z,)), D((H,)), D((1,)), D((H,)), D((1,)), D((2,)), D((1,)), D((1,)),
         ],
-        compiler_params=pltpu.CompilerParams(collective_id=0, has_side_effects=True, vmem_limit_bytes=61 << 20),
+        compiler_params=pltpu.CompilerParams(collective_id=0, has_side_effects=True, vmem_limit_bytes=53 << 20),
         cost_estimate=pl.CostEstimate(flops=1_300_000_000, bytes_accessed=2_300_000, transcendentals=0),
         name="exchange",
     )(orbitals, kern, basis)

time: 60.9 us -> 59.2 us (0.972)
  Pallas kernels: 59.2 us -> 57.7 us
    pallas_call x1, Pallas kernels: 59.2 us -> 57.7 us  [body(): pl.pallas_call(kernel, out_shape=jax.ShapeDtypeStruct((PIECE, 2, WIDTH //...]
    unnamed x1 -> x3, local copies, waits for them, and re-layouts: 1.47 us -> 1.39 us
where the time goes in v3:
time: 59.2 us; the launch traced here: 59.1 us
  Pallas kernels  57.7 us (97%)
  local copies, waits for them, and re-layouts  1.39 us (2%)
    pallas_call x1, Pallas kernels, body(): pl.pallas_call(kernel, out_shape=jax.ShapeDtypeStruct((PIECE, 2, WIDTH //...  57.7 us
    unnamed x3, local copies, waits for them, and re-layouts  1.39 us

profile of v3, /device:TPU:1, one launch (start us, length us, event | category | flops | bytes accessed | tf_op | source)
XLA Modules:
  0.0 59.1 jit_solution(18280615196319557726)
XLA Ops:
  0.0 0.0 copy-start
  0.0 0.8 %copy-done = bf16[32,2,256]{2,1,0:T(2,128)(2,1)S(1)} copy-done((bf16[32,2,256]{2,1,0:T(2,128)(2,1)S(1)}, bf16[32,2,256]{2,1,0:T(2,128)(2,1)}, u32[]{:S(2)}) %copy-start) | copy-done | bytes 32792
  0.8 57.7 %exchange.1 = f32[32,2,256]{2,1,0:T(2,128)S(1)} custom-call(bf16[32,2,256]{2,1,0:T(2,128)(2,1)S(1)} %copy-done, bf16[256,2048]{1,0:T(8,128)(2,1)} %kernel_ref.1, bf16[256,2048]{1,0:T(8,128)(2,1)} %basis_ref.1), custom_call_target="tpu_custom_call" | custom-call | flops 1300000000 | bytes 2300000 | tf_op jit(solution)/shard_map/exchange/pallas_call | solution.py:253
  58.4 0.6 %copy.5 = f32[32,2,256]{2,1,0:T(2,128)} copy(f32[32,2,256]{2,1,0:T(2,128)S(1)} %exchange.1) | data formatting | bytes 131072
Async XLA Ops:
  0.0 0.8 %copy-start = (bf16[32,2,256]{2,1,0:T(2,128)(2,1)S(1)}, bf16[32,2,256]{2,1,0:T(2,128)(2,1)}, u32[]{:S(2)}) copy-start(bf16[32,2,256]{2,1,0:T(2,128)(2,1)} %orb_ref.1) | copy-start | bytes 98308

commit v4 on v3

--- a/solution.py
+++ b/solution.py
@@ -1,3 +1,5 @@
+import functools
+
 import jax
 import jax.numpy as jnp
 from jax import lax
@@ -36,20 +38,25 @@
     def at_row(a, b, c):
         return (a * Z + b) * X + c
 
+    @functools.cache
     def z_dev(d):
         return {"row": at_row(yl, (z + d) % Z, x)}
 
+    @functools.cache
     def x_dev(e):
         return {"row": at_row(yl, z, (x + e) % X)}
 
     y_dev = {"row": at_row(1 - yl, z, x)}
 
+    @functools.cache
     def xy_dev(n):
         return {"row": at_row((yl + n // X) % Y, z, (x + n % X) % X)}
 
+    @functools.cache
     def c_at(dh, dk):
         return ((h + dh) % H) * K + (k + dk) % K
 
+    @functools.cache
     def c_dev(dh, dk):
         return {"col": c_at(dh, dk)}
 
@@ -81,8 +88,13 @@
 
     HALVES = pl.ds(0, 256), pl.ds(256, 256)
 
+    places = {}
+
     def block(y_at, d, e=0):
-        return col.at[at_row(y_at, (z - d + Z) % Z, (x - e + X) % X)]
+        other = y_at is not yl
+        if (other, d, e) not in places:
+            places[other, d, e] = at_row(1 - yl if other else yl, (z - d + Z) % Z, (x - e + X) % X)
+        return col.at[places[other, d, e]]
 
     own = col.at[row]
     send(own, own, 0, yr.at[0], y_dev)

time: 59.2 us -> 59.2 us (level)
  no operation moved by 1% of the time
where the time goes in v4:
time: 59.2 us; the launch traced here: 59.1 us
  Pallas kernels  57.7 us (97%)
  local copies, waits for them, and re-layouts  1.39 us (2%)
    pallas_call x1, Pallas kernels, body(): pl.pallas_call(kernel, out_shape=jax.ShapeDtypeStruct((PIECE, 2, WIDTH //...  57.7 us
    unnamed x3, local copies, waits for them, and re-layouts  1.39 us

profile of v4, /device:TPU:1, one launch (start us, length us, event | category | flops | bytes accessed | tf_op | source)
XLA Modules:
  0.0 59.1 jit_solution(18280615196319557726)
XLA Ops:
  0.0 0.0 copy-start
  0.0 0.8 %copy-done = bf16[32,2,256]{2,1,0:T(2,128)(2,1)S(1)} copy-done((bf16[32,2,256]{2,1,0:T(2,128)(2,1)S(1)}, bf16[32,2,256]{2,1,0:T(2,128)(2,1)}, u32[]{:S(2)}) %copy-start) | copy-done | bytes 32792
  0.8 57.7 %exchange.1 = f32[32,2,256]{2,1,0:T(2,128)S(1)} custom-call(bf16[32,2,256]{2,1,0:T(2,128)(2,1)S(1)} %copy-done, bf16[256,2048]{1,0:T(8,128)(2,1)} %kernel_ref.1, bf16[256,2048]{1,0:T(8,128)(2,1)} %basis_ref.1), custom_call_target="tpu_custom_call" | custom-call | flops 1300000000 | bytes 2300000 | tf_op jit(solution)/shard_map/exchange/pallas_call | solution.py:265
  58.4 0.6 %copy.5 = f32[32,2,256]{2,1,0:T(2,128)} copy(f32[32,2,256]{2,1,0:T(2,128)S(1)} %exchange.1) | data formatting | bytes 131072
Async XLA Ops:
  0.0 0.8 %copy-start = (bf16[32,2,256]{2,1,0:T(2,128)(2,1)S(1)}, bf16[32,2,256]{2,1,0:T(2,128)(2,1)}, u32[]{:S(2)}) copy-start(bf16[32,2,256]{2,1,0:T(2,128)(2,1)} %orb_ref.1) | copy-start | bytes 98308

commit v5 on v3

--- a/solution.py
+++ b/solution.py
@@ -13,13 +13,12 @@
 POINTS = COLS * PIECE
 BAND = X * PIECE
 HOPS = (0, 1, 7, 2, 6, 3, 5, 4)
-FAR = 4
+OVER_Y = (2, 6, 3, 5, 4)
 SCHEDULE = (
-    "s0", "t0", "B", "s1", "s7", "c0", "s2", "s6", "c1", "s3", "s5", "R",
-    "c7", "s4", "Z", "r0", "c2", "c6", "r1", "r7", "I", "c3", "n0", "c5",
-    "r2", "f0", "r6", "n1", "c4", "t1", "t7", "n7", "t4", "t2", "r3", "n2",
-    "t6", "r5", "n6", "t3", "t5", "f1", "r4", "f7", "n3", "n5", "f2", "n4",
-    "f6", "f3", "f5", "f4",
+    "s0", "t0", "B", "s1", "s7", "c0", "Z", "s2", "s6", "c1", "s3", "s5", "R", "c7",
+    "s4", "r0", "c2", "c6", "t1", "t7", "r1", "r7", "t2", "t6", "c3", "t3", "I", "n0",
+    "c5", "t5", "r2", "f0", "r6", "n1", "c4", "t4", "n7", "r3", "n2", "r5", "n6", "r4",
+    "f1", "f7", "n3", "n5", "f2", "n4", "f6", "f3", "f5", "f4",
 )
 BF, F32 = jnp.bfloat16, jnp.float32
 
@@ -80,6 +79,7 @@
         pltpu.make_async_copy(like, like, arrival).wait()
 
     HALVES = pl.ds(0, 256), pl.ds(256, 256)
+    OVER = pl.ds(0, 128), pl.ds(128, 384)
 
     def block(y_at, d, e=0):
         return col.at[at_row(y_at, (z - d + Z) % Z, (x - e + X) % X)]
@@ -98,8 +98,8 @@
             arrived(b, zr.at[d])
         for e in (1, 3):
             send(b, b, 2, xr.at[d], x_dev(e))
-        if d == FAR:
-            send(b, b, 0, yr.at[1], y_dev)
+        if d in OVER_Y:
+            send(b, b, 0, yr.at[d], y_dev)
 
     def cross(d):
         arrived(col.at[pl.ds(0, 2)], xr.at[d])
@@ -107,7 +107,7 @@
             half = block(yl, d, e).at[:, HALVES[n]]
             send(half, half, 3, xr3.at[d], x_dev(e))
         for e in (1, 3):
-            half = block(yl, d, e).at[:, HALVES[0]]
+            half = block(yl, d, e).at[:, OVER[0]]
             send(half, half, 4, lr.at[d], y_dev)
 
     def relay(d):
@@ -117,13 +117,13 @@
 
     def fan():
         b = block(1 - yl, 0)
-        for d in HOPS[1:-1]:
+        for d in [d for d in HOPS[1:] if d not in OVER_Y]:
             send(b, b, 1, zr2.at[d], z_dev(d))
 
     def spread2(d):
         b = block(1 - yl, d)
-        arrived(b, yr.at[d // FAR] if d in (0, FAR) else zr2.at[d])
-        half = b.at[:, HALVES[1]]
+        arrived(b, yr.at[d] if d == 0 or d in OVER_Y else zr2.at[d])
+        half = b.at[:, OVER[1]]
         for e in (1, 3):
             send(half, half, 6, lr.at[d], x_dev(e))
 
@@ -236,11 +236,11 @@
         sl = slice(q % 2 * 128, q % 2 * 128 + 128)
         out_ref[0:16, q // 2, sl] = jnp.where(low, a, pltpu.roll(b, 64, 1))
         out_ref[16:32, q // 2, sl] = jnp.where(low, pltpu.roll(a, 64, 1), b)
-    arrived(col.at[pl.ds(0, 9)], sent.at[0])
-    arrived(col.at[pl.ds(0, 13)], sent.at[1])
+    arrived(col.at[pl.ds(0, Z + len(OVER_Y))], sent.at[0])
+    arrived(col.at[pl.ds(0, 14 - len(OVER_Y))], sent.at[1])
     arrived(col.at[pl.ds(0, 16)], sent.at[2])
-    for n in (3, 4, 5, 6):
-        arrived(col.at[pl.ds(0, 8)], sent.at[n])
+    for n, blocks in enumerate((8, 4, 8, 12)):
+        arrived(col.at[pl.ds(0, blocks)], sent.at[3 + n])
     arrived(pairs, sent.at[7])
     arrived(part, sent.at[8])
     arrived(xpart, sent.at[9])
@@ -260,7 +260,7 @@
             V((1024, 512), BF), V((POINTS, WIDTH), F32), V((H, K, 128, 128), F32), V((H, 128, 128), F32), V((H, 128, 128), BF),
             V((H - 1, 128, 128), BF), V((Y, Z, X, 16, 128), F32), V((Y, Z, X, 16, 128), BF), V((2, X * Y - 1, Z // 2, 16, 128), BF),
             V((Z, 16, 128), F32), V((Z, 16, 128), F32), V((COLS, 16, 128), F32),
-            D((3,)), D((12,)), D((Z,)), D((Z,)), D((Z,)), D((Z,)), D((2,)), D((Z,)), D((H,)), D((1,)), D((H,)), D((1,)), D((2,)), D((1,)), D((1,)),
+            D((3,)), D((12,)), D((Z,)), D((Z,)), D((Z,)), D((Z,)), D((Z,)), D((Z,)), D((H,)), D((1,)), D((H,)), D((1,)), D((2,)), D((1,)), D((1,)),
         ],
         compiler_params=pltpu.CompilerParams(collective_id=0, has_side_effects=True, vmem_limit_bytes=53 << 20),
         cost_estimate=pl.CostEstimate(flops=1_300_000_000, bytes_accessed=2_300_000, transcendentals=0),

time: 59.2 us -> 59.3 us (level)
  no operation moved by 1% of the time
where the time goes in v5:
time: 59.3 us; the launch traced here: 59.2 us
  Pallas kernels  57.8 us (97%)
  local copies, waits for them, and re-layouts  1.39 us (2%)
    pallas_call x1, Pallas kernels, body(): pl.pallas_call(kernel, out_shape=jax.ShapeDtypeStruct((PIECE, 2, WIDTH //...  57.8 us
    unnamed x3, local copies, waits for them, and re-layouts  1.39 us

profile of v5, /device:TPU:1, one launch (start us, length us, event | category | flops | bytes accessed | tf_op | source)
XLA Modules:
  0.0 59.2 jit_solution(9123752528172540343)
XLA Ops:
  0.0 0.0 copy-start
  0.0 0.8 %copy-done = bf16[32,2,256]{2,1,0:T(2,128)(2,1)S(1)} copy-done((bf16[32,2,256]{2,1,0:T(2,128)(2,1)S(1)}, bf16[32,2,256]{2,1,0:T(2,128)(2,1)}, u32[]{:S(2)}) %copy-start) | copy-done | bytes 32792
  0.8 57.8 %exchange.1 = f32[32,2,256]{2,1,0:T(2,128)S(1)} custom-call(bf16[32,2,256]{2,1,0:T(2,128)(2,1)S(1)} %copy-done, bf16[256,2048]{1,0:T(8,128)(2,1)} %kernel_ref.1, bf16[256,2048]{1,0:T(8,128)(2,1)} %basis_ref.1), custom_call_target="tpu_custom_call" | custom-call | flops 1300000000 | bytes 2300000 | tf_op jit(solution)/shard_map/exchange/pallas_call | solution.py:253
  58.5 0.6 %copy.5 = f32[32,2,256]{2,1,0:T(2,128)} copy(f32[32,2,256]{2,1,0:T(2,128)S(1)} %exchange.1) | data formatting | bytes 131072
Async XLA Ops:
  0.0 0.8 %copy-start = (bf16[32,2,256]{2,1,0:T(2,128)(2,1)S(1)}, bf16[32,2,256]{2,1,0:T(2,128)(2,1)}, u32[]{:S(2)}) copy-start(bf16[32,2,256]{2,1,0:T(2,128)(2,1)} %orb_ref.1) | copy-start | bytes 98308
